TPU v7x, 32 devices: a whole 2x2x4 slice. The times are simulated.
32 devices in a mesh: rep: 2 (over x), fsdp: 4 (over z), ctx: 4 (over y, core).
Axes of the slice: x: 2, y: 2, z: 4, core: 2. Of those that a mesh axis runs over, the one named last changes fastest.
Arguments:
- inputs: bfloat16 [8, 1024, 2048], P(('rep', 'fsdp'), 'ctx'), may hold values from -6 to 6
- prefix: int32 [8], P(('rep', 'fsdp')), may hold values from 102 to 512
- joined_weight: bfloat16 [2048, 6144], P(('fsdp', 'ctx')), may hold values from -0.125 to 0.125
- query_bias: bfloat16 [2048], P(('fsdp', 'ctx')), may hold values from -3 to 3
- value_bias: bfloat16 [2048], P(('fsdp', 'ctx')), may hold values from -3 to 3
- dense_weight: bfloat16 [2048, 2048], P(('fsdp', 'ctx')), may hold values from -0.5 to 0.5
- dense_bias: bfloat16 [2048], P(('fsdp', 'ctx')), may hold values from -2 to 2
- expand_weight: bfloat16 [2048, 8192], P(('fsdp', 'ctx')), may hold values from -0.125 to 0.125
- expand_bias: bfloat16 [8192], P(('fsdp', 'ctx')), may hold values from -3 to 3
- shrink_weight: bfloat16 [8192, 2048], P(('fsdp', 'ctx')), may hold values from -0.0625 to 0.0625
- shrink_bias: bfloat16 [2048], P(('fsdp', 'ctx')), may hold values from -2 to 2
- first_gain: bfloat16 [2048], P(('fsdp', 'ctx')), may hold values from 0.5 to 1.5
- first_shift: bfloat16 [2048], P(('fsdp', 'ctx')), may hold values from -2 to 2
- second_gain: bfloat16 [2048], P(('fsdp', 'ctx')), may hold values from 0.5 to 1.5
- second_shift: bfloat16 [2048], P(('fsdp', 'ctx')), may hold values from -2 to 2
- cotangent: bfloat16 [8, 1024, 2048], P(('rep', 'fsdp'), 'ctx'), may hold values from -6 to 6
Outputs:
- layer_output: float32 [8, 1024, 2048], P(('rep', 'fsdp'), 'ctx')
- input_gradient: float32 [8, 1024, 2048], P(('rep', 'fsdp'), 'ctx')
- joined_gradient: float32 [2048, 6144], P(('fsdp', 'ctx'))
- query_bias_gradient: float32 [2048], P(('fsdp', 'ctx'))
- value_bias_gradient: float32 [2048], P(('fsdp', 'ctx'))
- dense_gradient: float32 [2048, 2048], P(('fsdp', 'ctx'))
- dense_bias_gradient: float32 [2048], P(('fsdp', 'ctx'))
- expand_gradient: float32 [2048, 8192], P(('fsdp', 'ctx'))
- expand_bias_gradient: float32 [8192], P(('fsdp', 'ctx'))
- shrink_gradient: float32 [8192, 2048], P(('fsdp', 'ctx'))
- shrink_bias_gradient: float32 [2048], P(('fsdp', 'ctx'))
- first_gain_gradient: float32 [2048], P(('fsdp', 'ctx'))
- first_shift_gradient: float32 [2048], P(('fsdp', 'ctx'))
- second_gain_gradient: float32 [2048], P(('fsdp', 'ctx'))
- second_shift_gradient: float32 [2048], P(('fsdp', 'ctx'))
All inputs are finite; a program needn't handle non-finite values.
Results may differ from a plain program's by a relative error of at most 0.014.
Values may be sent and summed in bfloat16 or wider, within the bound.
No kernel may reach another device: no remote copies, remote signals or barrier semaphores. Data moves between devices by JAX's collectives and lax.ppermute only.
A program may use at most 576 MiB of HBM per device.

v0:
```python
import jax
import jax.numpy as jnp
from jax import lax
from jax.sharding import PartitionSpec as P

H = 32
HD = 64
TP = ("rep", "ctx")
BF = jnp.bfloat16
F32 = jnp.float32


def dot(a, b, ca, cb):
    return lax.dot_general(a, b, (((ca,), (cb,)), ((), ())), preferred_element_type=F32)


def norm_stats(values):
    average = jnp.mean(values, axis=-1, keepdims=True)
    centred = values - average
    variance = jnp.mean(centred * centred, axis=-1, keepdims=True)
    inverse = lax.rsqrt(variance + 1e-05)
    return (centred * inverse, inverse)


def norm_back(normed, inverse, gain, grad):
    u = grad * gain
    mean_u = jnp.mean(u, axis=-1, keepdims=True)
    mean_un = jnp.mean(u * normed, axis=-1, keepdims=True)
    return (u - mean_u - normed * mean_un) * inverse


def gelu(values):
    return 0.5 * values * (1.0 + lax.erf(values * 0.7071067811865476))


def gelu_slope(values):
    density = jnp.exp(values * values * -0.5) * 0.3989422804014327
    return 0.5 * (1.0 + lax.erf(values * 0.7071067811865476)) + values * density


def gather_tp(x):
    return lax.all_gather(x, TP, axis=0, tiled=True)


def scatter_tp(x):
    return lax.psum_scatter(x, TP, scatter_dimension=0, tiled=True)


def swap_tp(x):
    return lax.all_to_all(x, TP, 0, 0, tiled=True)


def attention_logits(q, k, heads, prefix):
    raw = jnp.einsum("sqhe,skhe->shqk", q, k, preferred_element_type=F32)
    length = k.shape[1]
    place = jnp.arange(length, dtype=jnp.int32)
    distance = jnp.abs(place[:, None] - place[None, :]).astype(F32)
    allowed = (place[None, None, :] <= place[None, :, None]) | (
        place[None, None, :] < prefix[:, None, None]
    )
    slopes = jnp.exp2(-8.0 * (heads.astype(F32) + 1.0) / H)
    logits = raw * 0.125 - slopes[None, :, None, None] * distance[None, None]
    return (logits, allowed[:, None])


def attention_forward(q, k, v, heads, prefix):
    logits, allowed = attention_logits(q, k, heads, prefix)
    masked = jnp.where(allowed, logits, -1e30)
    largest = jnp.max(masked, axis=-1, keepdims=True)
    exponent = jnp.exp(masked - largest)
    totals = jnp.sum(exponent, axis=-1, keepdims=True)
    probs = (exponent / totals).astype(BF)
    out = jnp.einsum("shqk,skhe->sqhe", probs, v, preferred_element_type=F32).astype(BF)
    return (out, largest + jnp.log(totals))


def attention_backward(q, k, v, lse, d_out, heads, prefix):
    logits, allowed = attention_logits(q, k, heads, prefix)
    probs = jnp.where(allowed, jnp.exp(logits - lse), 0.0)
    d_probs = jnp.einsum("sqhe,skhe->shqk", d_out, v, preferred_element_type=F32)
    weighted = jnp.sum(probs * d_probs, axis=-1, keepdims=True)
    d_raw = (probs * (d_probs - weighted) * 0.125).astype(BF)
    low = probs.astype(BF)
    d_q = jnp.einsum("shqk,skhe->sqhe", d_raw, k, preferred_element_type=F32).astype(BF)
    d_k = jnp.einsum("shqk,sqhe->skhe", d_raw, q, preferred_element_type=F32).astype(BF)
    d_v = jnp.einsum("shqk,sqhe->skhe", low, d_out, preferred_element_type=F32).astype(BF)
    return (d_q, d_k, d_v)


def shards(
    sizes,
    inputs,
    prefix,
    joined_weight,
    query_bias,
    value_bias,
    dense_weight,
    dense_bias,
    expand_weight,
    expand_bias,
    shrink_weight,
    shrink_bias,
    first_gain,
    first_shift,
    second_gain,
    second_shift,
    cotangent,
):
    R, F, C = sizes
    N = R * C
    rep = lax.axis_index("rep")
    ctx = lax.axis_index("ctx")
    S, T, D = inputs.shape
    t = S * T
    B = joined_weight.shape[0]
    FFB = shrink_weight.shape[0]
    FF = FFB * F * C
    E = FFB // R
    W = D // N
    aligned = B // R % HD == 0

    def split_columns(weight, groups):
        n = weight.shape[1] // groups
        if aligned or groups == 1:
            pieces = weight.reshape(B, groups, F, C, R, n // (F * C * R))
            mine = lax.dynamic_index_in_dim(pieces, rep, 4, keepdims=False)
            mine = mine.transpose(3, 0, 1, 2, 4)
        else:
            pieces = weight.reshape(B, groups, R, C, n // (C * R))
            mine = lax.dynamic_index_in_dim(pieces, rep, 2, keepdims=False)
            mine = mine.transpose(2, 0, 1, 3)
        return mine.reshape(C, B, groups * n // N)

    def columns(weight, groups):
        blocks = lax.all_to_all(split_columns(weight, groups), "ctx", 0, 0, tiled=True)
        return lax.all_gather(blocks.reshape(C * B, -1), "fsdp", axis=0, tiled=True)

    def join_columns(grad, groups):
        part = lax.psum_scatter(grad.astype(BF), "fsdp", scatter_dimension=0, tiled=True)
        blocks = lax.all_to_all(part.reshape(C, B, -1), "ctx", 0, 0, tiled=True)
        both = lax.all_gather(blocks, "rep", axis=0, tiled=False)
        if aligned or groups == 1:
            both = both.reshape(R, C, B, groups, F, -1).transpose(2, 3, 4, 1, 0, 5)
        else:
            both = both.reshape(R, C, B, groups, -1).transpose(2, 3, 0, 1, 4)
        return both.reshape(B, -1).astype(F32)

    def half_rows(weight):
        n = weight.shape[0] // R
        return lax.dynamic_slice_in_dim(weight, rep * n, n, 0)

    def join_rows(part):
        return lax.all_gather(part, "rep", axis=0, tiled=True).astype(F32)

    small = jnp.concatenate(
        [
            first_gain,
            first_shift,
            second_gain,
            second_shift,
            dense_bias,
            shrink_bias,
            query_bias,
            value_bias,
            expand_bias,
        ]
    )
    small = lax.all_gather(small, ("fsdp", "ctx"), axis=0, tiled=False).astype(F32)
    gain_one, shift_one, gain_two, shift_two, dbias, sbias, qbias, vbias = [
        small[:, i * B : (i + 1) * B].reshape(D) for i in range(8)
    ]
    ebias = small[:, 8 * B :].reshape(F, C, R, E)
    ebias = lax.dynamic_index_in_dim(
        lax.dynamic_index_in_dim(ebias, ctx, 1, False), rep, 1, False
    ).reshape(F * E)

    def my_features(vector):
        if aligned:
            v = vector.reshape(F, C, R, -1)
            return lax.dynamic_index_in_dim(
                lax.dynamic_index_in_dim(v, ctx, 1, False), rep, 1, False
            ).reshape(W)
        return lax.dynamic_slice_in_dim(vector, (rep * C + ctx) * W, W, 0)

    my_heads = my_features(jnp.repeat(jnp.arange(H, dtype=jnp.int32), HD)).reshape(-1, HD)[:, 0]
    prefix_all = lax.all_gather(prefix, "rep", axis=0, tiled=True)
    joined_cols = columns(joined_weight, 3)
    dense_rows = (
        lax.all_gather(half_rows(dense_weight), "fsdp", axis=0, tiled=True) if aligned else None
    )
    expand_cols = columns(expand_weight, 1)
    shrink_rows = lax.all_gather(half_rows(shrink_weight), "fsdp", axis=0, tiled=True)
    if aligned:
        dense_all = gather_tp(dense_rows)
    else:
        dense_all = lax.all_gather(dense_weight, ("fsdp", "ctx"), axis=0, tiled=True)

    def to_sequences(a):
        return a.reshape(R, C, S, T, -1).transpose(0, 2, 1, 3, 4).reshape(R * S, C * T, -1)

    def from_sequences(a):
        return a.reshape(R, S, C, T, -1).transpose(0, 2, 1, 3, 4).reshape(N * t, -1)

    start = inputs.astype(F32).reshape(t, D)
    n1, inv1 = norm_stats(start)
    a1 = (n1 * gain_one + shift_one).astype(BF)
    a1_all = gather_tp(a1)
    g = cotangent.reshape(t, D)
    g_all = gather_tp(g)
    qkv = dot(a1_all, joined_cols, 1, 0)
    q = (qkv[:, :W] + my_features(qbias)).astype(BF)
    k = qkv[:, W : 2 * W].astype(BF)
    v = (qkv[:, 2 * W :] + my_features(vbias)).astype(BF)
    heads = lambda a: to_sequences(a).reshape(R * S, C * T, W // HD, HD)
    q, k, v = (heads(q), heads(k), heads(v))
    out, lse = attention_forward(q, k, v, my_heads, prefix_all)
    o = swap_tp(from_sequences(out).reshape(N, t, W))
    o = o.transpose(1, 0, 2).reshape(t, D)
    midway = start + dot(o, dense_all, 1, 0) + dbias
    n2, inv2 = norm_stats(midway)
    a2 = (n2 * gain_two + shift_two).astype(BF)
    a2_all = gather_tp(a2)
    expanded = dot(a2_all, expand_cols, 1, 0) + ebias
    act = gelu(expanded).astype(BF)
    branch = scatter_tp(dot(act, shrink_rows, 1, 0).astype(BF))
    layer_output = midway + branch.astype(F32) + sbias
    g_float = g.astype(F32)
    d_act = dot(g_all, shrink_rows, 1, 1)
    d_exp = (d_act * gelu_slope(expanded)).astype(BF)
    d_a2 = scatter_tp(dot(d_exp, expand_cols, 1, 1).astype(BF)).astype(F32)
    shrink_grad = dot(act, g_all, 0, 0).astype(BF)
    expand_grad = dot(a2_all, d_exp, 0, 0)
    ebias_grad = jnp.sum(d_exp.astype(F32), axis=0)
    sbias_grad = jnp.sum(g_float, axis=0)
    d_mid = g_float + norm_back(n2, inv2, gain_two, d_a2)
    gain_two_grad = jnp.sum(d_a2 * n2, axis=0)
    shift_two_grad = jnp.sum(d_a2, axis=0)
    d_att = d_mid.astype(BF)
    dense_grad = dot(o, d_att, 0, 0)
    dbias_grad = jnp.sum(d_att.astype(F32), axis=0)
    d_o = dot(d_att, dense_all, 1, 1).astype(BF)
    d_o = swap_tp(d_o.reshape(t, N, W).transpose(1, 0, 2)).reshape(N * t, W)
    d_q, d_k, d_v = attention_backward(q, k, v, lse, heads(d_o), my_heads, prefix_all)
    d_qkv = jnp.concatenate(
        [from_sequences(a.reshape(R * S, C * T, W)) for a in (d_q, d_k, d_v)], axis=1
    )
    d_a1 = scatter_tp(dot(d_qkv, joined_cols, 1, 1).astype(BF)).astype(F32)
    joined_grad = dot(a1_all, d_qkv, 0, 0)
    qkv_bias_grad = jnp.sum(d_qkv.astype(F32), axis=0)
    input_gradient = d_mid + norm_back(n1, inv1, gain_one, d_a1)
    gain_one_grad = jnp.sum(d_a1 * n1, axis=0)
    shift_one_grad = jnp.sum(d_a1, axis=0)
    shrink_out = join_rows(lax.psum_scatter(shrink_grad, "fsdp", scatter_dimension=0, tiled=True))
    expand_out = join_columns(expand_grad, 1)
    if aligned:
        part = scatter_tp(dense_grad.astype(BF))
        dense_out = join_rows(lax.psum_scatter(part, "fsdp", scatter_dimension=0, tiled=True))
    else:
        part = lax.psum_scatter(
            dense_grad.astype(BF), ("fsdp", "ctx"), scatter_dimension=0, tiled=True
        )
        dense_out = lax.psum(part, "rep").astype(F32)
    joined_out = join_columns(joined_grad, 3)

    def spread(vector, width):
        if aligned or width != D:
            full = jnp.zeros((F, C, R, width // (F * C * R)), F32)
            full = lax.dynamic_update_slice(full, vector.reshape(F, 1, 1, -1), (0, ctx, rep, 0))
        else:
            full = lax.dynamic_update_slice_in_dim(
                jnp.zeros((width,), F32), vector, (rep * C + ctx) * W, 0
            )
        return full.reshape(F * C, -1)

    tokens = [gain_one_grad, shift_one_grad, gain_two_grad, shift_two_grad, dbias_grad, sbias_grad]
    rows = [a.reshape(F * C, B) for a in tokens]
    rows += [
        spread(qkv_bias_grad[:W], D),
        spread(qkv_bias_grad[2 * W :], D),
        spread(ebias_grad, FF),
    ]
    little = jnp.concatenate(rows, axis=1)
    little = lax.psum(
        lax.psum_scatter(little, ("fsdp", "ctx"), scatter_dimension=0, tiled=True), "rep"
    ).reshape(-1)
    (
        gain_one_out,
        shift_one_out,
        gain_two_out,
        shift_two_out,
        dbias_out,
        sbias_out,
        qbias_out,
        vbias_out,
    ) = [little[i * B : (i + 1) * B] for i in range(8)]
    ebias_out = little[8 * B :]
    return (
        layer_output.reshape(S, T, D),
        input_gradient.reshape(S, T, D),
        joined_out,
        qbias_out,
        vbias_out,
        dense_out,
        dbias_out,
        expand_out,
        ebias_out,
        shrink_out,
        sbias_out,
        gain_one_out,
        shift_one_out,
        gain_two_out,
        shift_two_out,
    )


def solution(mesh):
    sizes = (mesh.shape["rep"], mesh.shape["fsdp"], mesh.shape["ctx"])
    tokens = P(("rep", "fsdp"), "ctx", None)
    matrix = P(("fsdp", "ctx"), None)
    vector = P(("fsdp", "ctx"))
    in_specs = (
        tokens,
        P(("rep", "fsdp")),
        matrix,
        vector,
        vector,
        matrix,
        vector,
        matrix,
        vector,
        matrix,
        vector,
        vector,
        vector,
        vector,
        vector,
        tokens,
    )
    out_specs = (
        tokens,
        tokens,
        matrix,
        vector,
        vector,
        matrix,
        vector,
        matrix,
        vector,
        matrix,
        vector,
        vector,
        vector,
        vector,
        vector,
    )

    def step(*arrays):
        return shards(sizes, *arrays)

    return jax.shard_map(step, mesh=mesh, in_specs=in_specs, out_specs=out_specs, check_vma=False)
```

profile of v0, /device:TPU:0, one launch (start us, length us, event | category | flops | bytes accessed | tf_op | source)
XLA Modules:
  0.0 1312.8 jit_solution(1803940489215172898)
XLA Ops:
  33.2 21.2 %all-gather.4 = bf16[16,1,1536]{2,1,0:T(2,128)(2,1)S(1)} all-gather(bf16[1,1,1536]{2,1,0:T(2,128)(2,1)S(1)} %reshape.335), channel_id=2, replica_groups=mesh['rep'=2,'fsdp'=4,'ctx'=4] {'fsdp','ctx'}, dimensions={0}, use_global_device_ids=true | all-gather | bytes 52224 | tf_op jit(solution)/shard_map/all_gather | solution.py:168
  106.2 55.5 %all-gather.17.cloned.1.call-done = bf16[2048,2048]{1,0:T(8,128)(2,1)} async-done(((bf16[256,2048]{1,0:T(8,128)(2,1)}), bf16[2048,2048]{1,0:T(8,128)(2,1)}) %all-gather.17.cloned.1.call-update) | async-done | bytes 8388624 | tf_op jit(solution)/shard_map/all_gather | solution.py:42
  200.1 22.8 %select_reduce_fusion = (f32[2,4,1024]{2,1,0:T(4,128)S(1)}, f32[2,4,1024,1024]{2,3,1,0:T(8,128)}) fusion(f32[4,1024,1024]{1,2,0:T(8,128)} %broadcast_multiply_fusion, pred[2,1024,1024]{1,2,0:T(8,128)(4,1)} %broadcast_or_fusion, bf16[2,1024,4,64]{1,3,2,0:T(8,128)(2,1)} %copy.112, bf16[2,1024,4,64]{1,3,2,0:T(8,128)(2,1)} %copy.113), kind=kOutput, calls=%fused_computation.8 | convolution fusion | flops 1107288064 | bytes 54558720 | tf_op jit(solution)/shard_map/sqhe,skhe->shqk/dot_general | solution.py:54
  222.9 19.0 %fusion.4 = f32[2,4,1024]{2,1,0:T(4,128)S(1)} fusion(f32[2,4,1024,1024]{2,3,1,0:T(8,128)} %get-tuple-element.92, f32[2,4,1024]{2,1,0:T(4,128)S(1)} %get-tuple-element.91, f32[4,1024,1024]{1,2,0:T(8,128)} %broadcast_multiply_fusion, pred[2,1024,1024]{1,2,0:T(8,128)(4,1)S(1)} %copy-done.2), kind=kLoop, calls=%fused_computation.9 | loop fusion | flops 41934848 | bytes 52494336 | tf_op jit(solution)/shard_map/reduce_sum | solution.py:71
  241.9 19.5 %fusion.72 = bf16[2,1024,4,64]{1,3,2,0:T(8,128)(2,1)S(1)} fusion(bf16[2,1024,4,64]{1,3,2,0:T(8,128)(2,1)S(1)} %copy-done.13, f32[2,4,1024,1024]{2,3,1,0:T(8,128)} %get-tuple-element.92, f32[2,4,1024]{2,1,0:T(4,128)S(1)} %fusion.4, f32[2,4,1024]{2,1,0:T(4,128)S(1)} %get-tuple-element.91, f32[4,1024,1024]{1,2,0:T(8,128)} %broadcast_multiply_fusion, ...), kind=kOutput, calls=%fused_computation.92 | convolution fusion | flops 1124597760 | bytes 54591488 | tf_op jit(solution)/shard_map/shqk,skhe->sqhe/dot_general | solution.py:73
  267.1 17.7 %all_to_all.31 = bf16[8,256,256]{1,2,0:T(8,128)(2,1)} all-to-all(bf16[8,256,256]{1,2,0:T(8,128)(2,1)S(1)} %copy.117), channel_id=1, replica_groups=mesh['rep'=2,'fsdp'=4,'ctx'=4] {'rep','ctx'}, dimensions={0} | all-to-all | bytes 2097152 | tf_op jit(solution)/shard_map/all_to_all | solution.py:50
  300.7 55.3 %all-gather.25.cloned.1.call-done = bf16[2048,2048]{1,0:T(8,128)(2,1)} async-done(((bf16[256,2048]{1,0:T(8,128)(2,1)}), bf16[2048,2048]{1,0:T(8,128)(2,1)}) %all-gather.25.cloned.1.call-update) | async-done | bytes 8388624 | tf_op jit(solution)/shard_map/all_gather | solution.py:42
  355.9 15.9 %multiply_convert_fusion.1 = (bf16[2048,1024]{1,0:T(8,128)(2,1)}, f32[2048,1024]{1,0:T(8,128)}) fusion(f32[1024]{0:T(1024)S(1)} %bitcast.232, bf16[2048,2048]{1,0:T(8,128)(2,1)} %all-gather.25.cloned.1.call-done, bf16[2048,1024]{1,0:T(8,128)(2,1)} %all-gather.27.cloned.1.call-done), kind=kOutput, calls=%fused_computation.22 | convolution fusion | flops 8602517504 | bytes 25169920 | tf_op jit(solution)/shard_map/dot_general | solution.py:14
  371.8 66.5 %all-gather.29.cloned.1.call-done = bf16[1024,2048]{1,0:T(8,128)(2,1)} async-done(((bf16[256,2048]{1,0:T(8,128)(2,1)}), bf16[1024,2048]{1,0:T(8,128)(2,1)}) %all-gather.29.cloned.1.call-update) | async-done | bytes 4194320 | tf_op jit(solution)/shard_map/all_gather | solution.py:192
  438.3 54.8 %all-gather.33.cloned.1.call-done = bf16[1,2048,2048]{2,1,0:T(8,128)(2,1)} async-done(((bf16[1,256,2048]{2,1,0:T(8,128)(2,1)}), bf16[1,2048,2048]{2,1,0:T(8,128)(2,1)}) %all-gather.33.cloned.1.call-update) | async-done | bytes 8388624 | tf_op jit(solution)/shard_map/all_gather | solution.py:42
  493.1 17.0 %convert_reduce_fusion = (f32[1024]{0:T(1024)}, bf16[2048,1024]{1,0:T(8,128)(2,1)S(1)}) fusion(f32[2048,1024]{1,0:T(8,128)} %get-tuple-element.96, f32[1024]{0:T(1024)S(1)} %bitcast.233, bf16[1024,2048]{1,0:T(8,128)(2,1)} %all-gather.29.cloned.1.call-done, bf16[1,2048,2048]{2,1,0:T(8,128)(2,1)} %all-gather.33.cloned.1.call-done), kind=kOutput, calls=%fused_computation.21 | convolution fusion | flops 8617196544 | bytes 25174016 | tf_op jit(solution)/shard_map/dot_general | solution.py:14
  552.3 42.2 %reduce-scatter.11.cloned.1.call-done = bf16[256,2048]{1,0:T(8,128)(2,1)} async-done(((bf16[2048,2048]{1,0:T(8,128)(2,1)}), bf16[256,2048]{1,0:T(8,128)(2,1)}) %reduce-scatter.11.cloned.1.call-update) | async-done | bytes 1048592 | tf_op jit(solution)/shard_map/reduce_scatter | solution.py:46
  597.3 72.2 %reduce-scatter.9.cloned.1.call-done = bf16[256,2048]{1,0:T(8,128)(2,1)} async-done(((bf16[2048,2048]{1,0:T(8,128)(2,1)}), bf16[256,2048]{1,0:T(8,128)(2,1)}) %reduce-scatter.9.cloned.1.call-update) | async-done | bytes 1048592 | tf_op jit(solution)/shard_map/reduce_scatter | solution.py:46
  704.2 18.3 %fusion.63 = bf16[2,1024,4,64]{1,3,2,0:T(8,128)(2,1)S(1)} fusion(bf16[2,1024,4,64]{1,0,3,2:T(2,128)(2,1)S(1)} %reshape_reshape_transpose_reshape_reshape.3, f32[2,4,1024,1024]{2,3,1,0:T(8,128)} %get-tuple-element.92, f32[2,4,1024]{2,1,0:T(4,128)S(1)} %bitcast.221, f32[4,1024,1024]{1,2,0:T(8,128)} %broadcast_multiply_fusion, ...), kind=kOutput, calls=%fused_computation.89 | convolution fusion | flops 1116209152 | bytes 54558720 | tf_op jit(solution)/shard_map/shqk,sqhe->skhe/dot_general | solution.py:86
  738.1 55.8 %fusion.66 = bf16[2,1024,4,64]{1,3,2,0:T(8,128)(2,1)} fusion(bf16[2,1024,4,64]{1,3,2,0:T(8,128)(2,1)} %copy.112, f32[2,4,1024,1024]{2,3,1,0:T(8,128)} %fusion.74, f32[2,4,1024,1024]{2,3,1,0:T(8,128)} %get-tuple-element.92, f32[2,4,1024]{2,1,0:T(4,128)S(1)} %bitcast.222, f32[4,1024,1024]{1,2,0:T(8,128)} %broadcast_multiply_fusion, ...), kind=kOutput, calls=%fused_computation.90 | convolution fusion | flops 1183327232 | bytes 88113152 | tf_op jit(solution)/shard_map/shqk,sqhe->skhe/dot_general | solution.py:85
  797.6 54.7 %fusion.69 = bf16[2,1024,4,64]{1,3,2,0:T(8,128)(2,1)} fusion(bf16[2,1024,4,64]{1,3,2,0:T(8,128)(2,1)S(1)} %copy-done.16, f32[2,4,1024,1024]{2,3,1,0:T(8,128)} %fusion.74, f32[2,4,1024,1024]{2,3,1,0:T(8,128)} %get-tuple-element.92, f32[2,4,1024]{2,1,0:T(4,128)S(1)} %bitcast.223, f32[4,1024,1024]{1,2,0:T(8,128)} %broadcast_multiply_fusion, ...), kind=kOutput, calls=%fused_computation.91 | convolution fusion | flops 1183327232 | bytes 88113152 | tf_op jit(solution)/shard_map/shqk,skhe->sqhe/dot_general | solution.py:84
  887.5 18.8 %all_to_all.32 = bf16[4,128,1024]{2,1,0:T(8,128)(2,1)} all-to-all(bf16[4,128,1024]{2,1,0:T(8,128)(2,1)} %bitcast.220), channel_id=1, replica_groups=mesh['rep'=2,'fsdp'=4,'ctx'=4] {'ctx'}, dimensions={0} | all-to-all | bytes 2097152 | tf_op jit(solution)/shard_map/all_to_all | solution.py:140
  906.3 22.6 %reduce-scatter.15.cloned.1.call-done = bf16[512,768]{1,0:T(8,128)(2,1)} async-done(((bf16[2048,768]{1,0:T(8,128)(2,1)}), bf16[512,768]{1,0:T(8,128)(2,1)}) %reduce-scatter.15.cloned.1.call-update) | async-done | bytes 786448 | tf_op jit(solution)/shard_map/reduce_scatter | solution.py:139
  945.1 58.4 %reduce-scatter.13.cloned.1.call-done = bf16[256,2048]{1,0:T(8,128)(2,1)} async-done(((bf16[2048,2048]{1,0:T(8,128)(2,1)}), bf16[256,2048]{1,0:T(8,128)(2,1)}) %reduce-scatter.13.cloned.1.call-update) | async-done | bytes 1048592 | tf_op jit(solution)/shard_map/reduce_scatter | solution.py:46
  1006.7 71.9 %reduce-scatter.17.cloned.1.call-done = bf16[256,2048]{1,0:T(8,128)(2,1)} async-done(((bf16[2048,2048]{1,0:T(8,128)(2,1)}), bf16[256,2048]{1,0:T(8,128)(2,1)}) %reduce-scatter.17.cloned.1.call-update) | async-done | bytes 1048592 | tf_op jit(solution)/shard_map/reduce_scatter | solution.py:46
  1079.2 33.9 %all-gather.31.cloned.1.call-done = bf16[512,2048]{1,0:T(8,128)(2,1)} async-done(((bf16[256,2048]{1,0:T(8,128)(2,1)}), bf16[512,2048]{1,0:T(8,128)(2,1)}) %all-gather.31.cloned.1.call-update) | async-done | bytes 2097168 | tf_op jit(solution)/shard_map/all_gather | solution.py:153
  1117.3 30.4 %all-gather.37.cloned.1.call-done = bf16[8,128,1024]{2,1,0:T(8,128)(2,1)} async-done(((bf16[4,128,1024]{2,1,0:T(8,128)(2,1)}), bf16[8,128,1024]{2,1,0:T(8,128)(2,1)}) %all-gather.37.cloned.1.call-update) | async-done | bytes 2097168 | tf_op jit(solution)/shard_map/all_gather | solution.py:141
  1188.8 78.7 %all-reduce.4.cloned.1.call-done = f32[16,1536]{1,0:T(8,128)} async-done(((f32[16,1536]{1,0:T(8,128)}), f32[16,1536]{1,0:T(8,128)}) %all-reduce.4.cloned.1.call-update) | async-done | bytes 98320
  1275.1 20.9 %reduce-scatter.19.cloned.1.call-done = bf16[64,2048]{1,0:T(8,128)(2,1)} async-done(((bf16[256,2048]{1,0:T(8,128)(2,1)}), bf16[64,2048]{1,0:T(8,128)(2,1)}) %reduce-scatter.19.cloned.1.call-update) | async-done | bytes 262160 | tf_op jit(solution)/shard_map/reduce_scatter | solution.py:257
  (277 shorter events, 352.8 us)
Async XLA Ops:
  7.2 286.6 %copy-start = (bf16[512,2048]{1,0:T(8,128)(2,1)S(1)}, bf16[512,2048]{1,0:T(8,128)(2,1)}, u32[]{:S(2)}) copy-start(bf16[512,2048]{1,0:T(8,128)(2,1)} %param.25) | copy-start | bytes 6291460
  7.2 50.6 %all-gather.21.cloned.1.call-start = ((), (), s32[]{:S(2)}) async-start(), calls=%async_computation.16 | async-start | bytes 1310720 | tf_op jit(solution)/shard_map/all_gather | solution.py:189
  9.1 97.1 %all-gather.19.cloned.1.call-start = ((), (), s32[]{:S(2)}) async-start(), calls=%async_computation.15 | async-start | bytes 3932160 | tf_op jit(solution)/shard_map/all_gather | solution.py:136
  31.3 130.4 %all-gather.17.cloned.1.call-start = ((), (), s32[]{:S(2)}) async-start(), calls=%async_computation.14 | async-start | bytes 9437184 | tf_op jit(solution)/shard_map/all_gather | solution.py:42
  57.7 227.1 %all-gather.23.cloned.1.call-start = ((), (), s32[]{:S(2)}) async-start(), calls=%async_computation.17 | async-start | bytes 9437184 | tf_op jit(solution)/shard_map/all_gather | solution.py:42
  69.2 24.2 %all-to-all-start.2 = ((bf16[4,128,1024]{1,2,0:T(8,128)(2,1)}), bf16[4,128,1024]{1,2,0:T(8,128)(2,1)}, u32[]{:S(2)}, u32[]{:S(2)}) async-start(bf16[4,128,1024]{1,2,0:T(8,128)(2,1)} %bitcast.209), calls=%async_computation.2 | async-start | bytes 2097152 | tf_op jit(solution)/shard_map/all_to_all | solution.py:135
  73.5 227.1 %all-gather.27.cloned.1.call-start = ((), (), s32[]{:S(2)}) async-start(), calls=%async_computation.19 | async-start | bytes 5242880 | tf_op jit(solution)/shard_map/all_gather | solution.py:136
  95.8 260.2 %all-gather.25.cloned.1.call-start = ((), (), s32[]{:S(2)}) async-start(), calls=%async_computation.18 | async-start | bytes 9437184 | tf_op jit(solution)/shard_map/all_gather | solution.py:42
  293.7 144.6 %all-gather.29.cloned.1.call-start = ((), (), s32[]{:S(2)}) async-start(), calls=%async_computation.20 | async-start | bytes 5242880 | tf_op jit(solution)/shard_map/all_gather | solution.py:192
  295.0 198.2 %all-gather.33.cloned.1.call-start = ((), (), s32[]{:S(2)}) async-start(), calls=%async_computation.30 | async-start | bytes 9437184 | tf_op jit(solution)/shard_map/all_gather | solution.py:42
  295.7 298.8 %reduce-scatter.11.cloned.1.call-start = ((), (), s32[]{:S(2)}) async-start(), calls=%async_computation.22 | async-start | bytes 9437184 | tf_op jit(solution)/shard_map/reduce_scatter | solution.py:46
  523.1 146.4 %reduce-scatter.9.cloned.1.call-start = ((), (), s32[]{:S(2)}) async-start(), calls=%async_computation.21 | async-start | bytes 9437184 | tf_op jit(solution)/shard_map/reduce_scatter | solution.py:46
  537.7 349.2 %reduce-scatter.23.cloned.1.call-start = ((), (), s32[]{:S(2)}) async-start(), calls=%async_computation.28 | async-start | bytes 5242880 | tf_op jit(solution)/shard_map/reduce_scatter | solution.py:253
  683.2 17.9 %all-to-all-start.3 = ((bf16[8,256,256]{1,2,0:T(8,128)(2,1)}), bf16[8,256,256]{1,2,0:T(8,128)(2,1)S(1)}, u32[]{:S(2)}, u32[]{:S(2)}) async-start(bf16[8,256,256]{1,2,0:T(8,128)(2,1)} %bitcast.29), calls=%async_computation.5 | async-start | bytes 2097152 | tf_op jit(solution)/shard_map/all_to_all | solution.py:50
  686.7 200.7 %reduce-scatter.21.cloned.1.call-start = ((), (), s32[]{:S(2)}) async-start(), calls=%async_computation.27 | async-start | bytes 5242880 | tf_op jit(solution)/shard_map/reduce_scatter | solution.py:139
  701.0 227.9 %reduce-scatter.15.cloned.1.call-start = ((), (), s32[]{:S(2)}) async-start(), calls=%async_computation.24 | async-start | bytes 3932160 | tf_op jit(solution)/shard_map/reduce_scatter | solution.py:139
  867.4 136.2 %reduce-scatter.13.cloned.1.call-start = ((), (), s32[]{:S(2)}) async-start(), calls=%async_computation.23 | async-start | bytes 9437184 | tf_op jit(solution)/shard_map/reduce_scatter | solution.py:46
  879.3 199.3 %reduce-scatter.17.cloned.1.call-start = ((), (), s32[]{:S(2)}) async-start(), calls=%async_computation.25 | async-start | bytes 9437184 | tf_op jit(solution)/shard_map/reduce_scatter | solution.py:46
  886.8 226.3 %all-gather.31.cloned.1.call-start = ((), (), s32[]{:S(2)}) async-start(), calls=%async_computation.29 | async-start | bytes 3145728 | tf_op jit(solution)/shard_map/all_gather | solution.py:153
  887.4 260.3 %all-gather.37.cloned.1.call-start = ((), (), s32[]{:S(2)}) async-start(), calls=%async_computation.32 | async-start | bytes 3145728 | tf_op jit(solution)/shard_map/all_gather | solution.py:141
  928.9 15.3 %all-to-all-start.4 = ((bf16[4,128,768]{2,1,0:T(8,128)(2,1)}), bf16[4,128,768]{2,1,0:T(8,128)(2,1)S(1)}, u32[]{:S(2)}, u32[]{:S(2)}) async-start(bf16[4,128,768]{2,1,0:T(8,128)(2,1)} %bitcast.224), calls=%async_computation.8 | async-start | bytes 1572864 | tf_op jit(solution)/shard_map/all_to_all | solution.py:140
  932.6 244.3 %all-gather.35.cloned.1.call-start = ((), (), s32[]{:S(2)}) async-start(), calls=%async_computation.31 | async-start | bytes 2359296 | tf_op jit(solution)/shard_map/all_gather | solution.py:141
  945.1 322.4 %all-reduce.4.cloned.1.call-start = ((), (), s32[]{:S(2)}) async-start(), calls=%async_computation.33 | async-start | bytes 196608
  1006.7 289.3 %reduce-scatter.19.cloned.1.call-start = ((), (), s32[]{:S(2)}) async-start(), calls=%async_computation.26 | async-start | bytes 1310720 | tf_op jit(solution)/shard_map/reduce_scatter | solution.py:257
  (44 other events, 1597.9 us)
Sparse Core Ops, SparseCore 0:
  10.2 30.7 all-gather.20
  43.1 63.0 all-gather.18
  108.6 53.0 all-gather.16
  163.5 54.3 all-gather.22
  219.9 80.7 all-gather.26
  303.0 52.9 all-gather.24
  357.5 80.7 all-gather.28
  440.2 52.9 all-gather.32
  523.2 71.2 reduce-scatter.10
  598.2 71.2 reduce-scatter.8
  671.8 76.7 reduce-scatter.22
  751.4 77.2 reduce-scatter.20
  867.5 61.3 reduce-scatter.14
  932.2 71.2 reduce-scatter.12
  1007.3 71.2 reduce-scatter.16
  1080.0 33.0 all-gather.30
  1114.5 33.1 all-gather.36
  1149.7 27.1 all-gather.34
  1180.3 87.1 all-reduce.3
  1269.8 26.1 reduce-scatter.18
where the time goes:
time: 1320 us; the launch traced here: 1310 us
  waiting for transfers between devices  699 us (53%)
  matrix products  322 us (24%)
  local copies, waits for them, and re-layouts  112 us (8%)
  blocking collectives  91.5 us (7%)
  other arithmetic  59.9 us (5%)
  between operations  15.9 us (1%)
    reduce_scatter x4, waiting for transfers between devices, scatter_tp(): return lax.psum_scatter(x, TP, scatter_dimension=0, tiled=True)  245 us
    all_gather x4, waiting for transfers between devices, gather_tp(): return lax.all_gather(x, TP, axis=0, tiled=True)  166 us
    dot_general x12, matrix products, dot(): lax.dot_general(a, b, (((ca,), (cb,)), ((), ())), preferred_element_type=...  138 us
    unnamed x21, waiting for transfers between devices  80.7 us
    all_gather x1, waiting for transfers between devices, shards(): lax.all_gather(half_rows(shrink_weight), 'fsdp', axis=0, tiled=True)  66.5 us
    dot_general x1, matrix products, attention_backward(): jnp.einsum('shqk,sqhe->skhe', d_raw, q, preferred_element_type=F32)  55.8 us
    dot_general x1, matrix products, attention_backward(): jnp.einsum('shqk,skhe->sqhe', d_raw, k, preferred_element_type=F32)  54.7 us
    all_gather x2, waiting for transfers between devices, join_columns(): both = lax.all_gather(blocks, 'rep', axis=0, tiled=False)  40.7 us
  transfers between devices with their start and end apart: 23, of which 18 were waited for; matrix products, arithmetic and copies ran while one was open for 35% of the time, Pallas kernels for 0%

commit v1 on v0

--- a/solution.py
+++ b/solution.py
@@ -189,7 +189,16 @@
         lax.all_gather(half_rows(dense_weight), "fsdp", axis=0, tiled=True) if aligned else None
     )
     expand_cols = columns(expand_weight, 1)
-    shrink_rows = lax.all_gather(half_rows(shrink_weight), "fsdp", axis=0, tiled=True)
+    value = half_rows(shrink_weight)
+    ways, here, step_2 = (lax.axis_size("fsdp"), lax.axis_index("fsdp"), value.shape[0])
+    line, have = (value, 1)
+    while have < ways:
+        line = jnp.concatenate(
+            [line, lax.ppermute(line, "fsdp", [(d, (d - have) % ways) for d in range(ways)])],
+            axis=0,
+        )
+        have = 2 * have
+    shrink_rows = jnp.roll(line, here * step_2, axis=0)
     if aligned:
         dense_all = gather_tp(dense_rows)
     else:

time: 1320 us -> 1280 us (0.970)
  waiting for transfers between devices: 699 us -> 638 us
    ppermute x0 -> x2, waiting for transfers between devices: none -> 112 us  [shards(): lax.ppermute(line, 'fsdp', [(d, (d - have) % ways) for d in range(ways)])]
    all_gather x4, waiting for transfers between devices: 166 us -> 55.5 us  [gather_tp(): return lax.all_gather(x, TP, axis=0, tiled=True)]
    all_gather x1 -> x0, waiting for transfers between devices: 66.5 us -> none  [shards(): lax.all_gather(half_rows(shrink_weight), 'fsdp', axis=0, tiled=True)]
    unnamed x122 -> x123, local copies, waits for them, and re-layouts: 28.3 us -> 39.3 us
    unnamed x21 -> x20, waiting for transfers between devices: 80.7 us -> 80.9 us
  transfers between devices with their start and end apart: 23 -> 24, of which waited for: 18 -> 16; matrix products, arithmetic and copies ran while one was open for 35% -> 37% of each run, Pallas kernels for 0% -> 0%
where the time goes in v1:
time: 1280 us; the launch traced here: 1270 us
  waiting for transfers between devices  638 us (50%)
  matrix products  323 us (25%)
  local copies, waits for them, and re-layouts  121 us (9%)
  blocking collectives  91.2 us (7%)
  other arithmetic  61.7 us (5%)
  starting transfers between devices  18.5 us (1%)
  between operations  15.6 us (1%)
    reduce_scatter x4, waiting for transfers between devices, scatter_tp(): return lax.psum_scatter(x, TP, scatter_dimension=0, tiled=True)  244 us
    dot_general x12, matrix products, dot(): lax.dot_general(a, b, (((ca,), (cb,)), ((), ())), preferred_element_type=...  140 us
    ppermute x2, waiting for transfers between devices, shards(): lax.ppermute(line, 'fsdp', [(d, (d - have) % ways) for d in range(ways)])  112 us
    unnamed x20, waiting for transfers between devices  80.9 us
    dot_general x1, matrix products, attention_backward(): jnp.einsum('shqk,sqhe->skhe', d_raw, q, preferred_element_type=F32)  55.8 us
    all_gather x4, waiting for transfers between devices, gather_tp(): return lax.all_gather(x, TP, axis=0, tiled=True)  55.5 us
    dot_general x1, matrix products, attention_backward(): jnp.einsum('shqk,skhe->sqhe', d_raw, k, preferred_element_type=F32)  55 us
    all_gather x2, waiting for transfers between devices, join_columns(): both = lax.all_gather(blocks, 'rep', axis=0, tiled=False)  40.7 us
  transfers between devices with their start and end apart: 24, of which 16 were waited for; matrix products, arithmetic and copies ran while one was open for 37% of the time, Pallas kernels for 0%

profile of v1, /device:TPU:0, one launch (start us, length us, event | category | flops | bytes accessed | tf_op | source)
XLA Modules:
  0.0 1269.6 jit_solution(397846810492300005)
XLA Ops:
  29.8 21.0 %all-gather.4 = bf16[16,1,1536]{2,1,0:T(2,128)(2,1)S(1)} all-gather(bf16[1,1,1536]{2,1,0:T(2,128)(2,1)S(1)} %reshape.335), channel_id=2, replica_groups=mesh['rep'=2,'fsdp'=4,'ctx'=4] {'fsdp','ctx'}, dimensions={0}, use_global_device_ids=true | all-gather | bytes 52224 | tf_op jit(solution)/shard_map/all_gather | solution.py:168
  87.2 19.2 %all-gather.18.cloned.1.call-done = bf16[2048,768]{1,0:T(8,128)(2,1)} async-done(((bf16[512,768]{1,0:T(8,128)(2,1)}), bf16[2048,768]{1,0:T(8,128)(2,1)}) %all-gather.18.cloned.1.call-update) | async-done | bytes 3145744 | tf_op jit(solution)/shard_map/all_gather | solution.py:136
  106.4 55.5 %all-gather.16.cloned.1.call-done = bf16[2048,2048]{1,0:T(8,128)(2,1)} async-done(((bf16[256,2048]{1,0:T(8,128)(2,1)}), bf16[2048,2048]{1,0:T(8,128)(2,1)}) %all-gather.16.cloned.1.call-update) | async-done | bytes 8388624 | tf_op jit(solution)/shard_map/all_gather | solution.py:42
  200.4 20.2 %select_reduce_fusion = (f32[2,4,1024]{2,1,0:T(4,128)S(1)}, f32[2,4,1024,1024]{2,3,1,0:T(8,128)}) fusion(f32[4,1024,1024]{1,2,0:T(8,128)} %broadcast_multiply_fusion, pred[2,1024,1024]{1,2,0:T(8,128)(4,1)S(1)} %broadcast_or_fusion, bf16[2,1024,4,64]{1,3,2,0:T(8,128)(2,1)} %copy.112, bf16[2,1024,4,64]{1,3,2,0:T(8,128)(2,1)} %copy.113), kind=kOutput, calls=%fused_computation.8 | convolution fusion | flops 1107288064 | bytes 54558720 | tf_op jit(solution)/shard_map/sqhe,skhe->shqk/dot_general | solution.py:54
  220.5 18.9 %fusion.4 = f32[2,4,1024]{2,1,0:T(4,128)S(1)} fusion(f32[2,4,1024,1024]{2,3,1,0:T(8,128)} %get-tuple-element.94, f32[2,4,1024]{2,1,0:T(4,128)S(1)} %get-tuple-element.93, f32[4,1024,1024]{1,2,0:T(8,128)} %broadcast_multiply_fusion, pred[2,1024,1024]{1,2,0:T(8,128)(4,1)S(1)} %broadcast_or_fusion), kind=kLoop, calls=%fused_computation.9 | loop fusion | flops 41934848 | bytes 52494336 | tf_op jit(solution)/shard_map/reduce_sum | solution.py:71
  239.4 19.5 %fusion.74 = bf16[2,1024,4,64]{1,3,2,0:T(8,128)(2,1)S(1)} fusion(bf16[2,1024,4,64]{1,3,2,0:T(8,128)(2,1)S(1)} %copy-done.12, f32[2,4,1024,1024]{2,3,1,0:T(8,128)} %get-tuple-element.94, f32[2,4,1024]{2,1,0:T(4,128)S(1)} %fusion.4, f32[2,4,1024]{2,1,0:T(4,128)S(1)} %get-tuple-element.93, f32[4,1024,1024]{1,2,0:T(8,128)} %broadcast_multiply_fusion, ...), kind=kOutput, calls=%fused_computation.95 | convolution fusion | flops 1124597760 | bytes 54591488 | tf_op jit(solution)/shard_map/shqk,skhe->sqhe/dot_general | solution.py:73
  264.6 17.7 %all_to_all.31 = bf16[8,256,256]{1,2,0:T(8,128)(2,1)} all-to-all(bf16[8,256,256]{1,2,0:T(8,128)(2,1)S(1)} %copy.117), channel_id=1, replica_groups=mesh['rep'=2,'fsdp'=4,'ctx'=4] {'rep','ctx'}, dimensions={0} | all-to-all | bytes 2097152 | tf_op jit(solution)/shard_map/all_to_all | solution.py:50
  298.0 23.9 %collective-permute-done = bf16[256,2048]{1,0:T(8,128)(2,1)S(1)} collective-permute-done((bf16[256,2048]{1,0:T(8,128)(2,1)S(1)}, bf16[256,2048]{1,0:T(8,128)(2,1)S(1)}, u32[]{:S(2)}, u32[]{:S(2)}) %collective-permute-start) | collective-permute-done | bytes 1048608 | tf_op jit(solution)/shard_map/ppermute | solution.py:197
  328.1 88.4 %collective-permute-done.1 = bf16[512,2048]{1,0:T(8,128)(2,1)} collective-permute-done((bf16[512,2048]{1,0:T(8,128)(2,1)}, bf16[512,2048]{1,0:T(8,128)(2,1)}, u32[]{:S(2)}, u32[]{:S(2)}) %collective-permute-start.1) | collective-permute-done | bytes 2097184 | tf_op jit(solution)/shard_map/ppermute | solution.py:197
  426.3 15.9 %multiply_convert_fusion.1 = (bf16[2048,1024]{1,0:T(8,128)(2,1)}, f32[2048,1024]{1,0:T(8,128)}) fusion(f32[1024]{0:T(1024)S(1)} %bitcast.230, bf16[2048,2048]{1,0:T(8,128)(2,1)} %all-gather.24.cloned.1.call-done, bf16[2048,1024]{1,0:T(8,128)(2,1)} %all-gather.26.cloned.1.call-done), kind=kOutput, calls=%fused_computation.22 | convolution fusion | flops 8602517504 | bytes 25169920 | tf_op jit(solution)/shard_map/dot_general | solution.py:14
  442.2 17.0 %convert_reduce_fusion = (f32[1024]{0:T(1024)}, bf16[2048,1024]{1,0:T(8,128)(2,1)S(1)}) fusion(f32[2048,1024]{1,0:T(8,128)} %get-tuple-element.98, f32[1024]{0:T(1024)S(1)} %bitcast.231, bf16[1,2048,2048]{2,1,0:T(8,128)(2,1)} %all-gather.30.cloned.1.call-done, bf16[2048,2048]{1,0:T(8,128)(2,1)} %constant_dynamic-update-slice_fusion, s32[]{:T(128)S(6)} %select_n.66), kind=kOutput, calls=%fused_computation.21 | convolution fusion | flops 8617196544 | bytes 25174020 | tf_op jit(solution)/shard_map/dot_general | solution.py:14
  501.4 42.1 %reduce-scatter.11.cloned.1.call-done = bf16[256,2048]{1,0:T(8,128)(2,1)} async-done(((bf16[2048,2048]{1,0:T(8,128)(2,1)}), bf16[256,2048]{1,0:T(8,128)(2,1)}) %reduce-scatter.11.cloned.1.call-update) | async-done | bytes 1048592 | tf_op jit(solution)/shard_map/reduce_scatter | solution.py:46
  547.0 71.7 %reduce-scatter.9.cloned.1.call-done = bf16[256,2048]{1,0:T(8,128)(2,1)} async-done(((bf16[2048,2048]{1,0:T(8,128)(2,1)}), bf16[256,2048]{1,0:T(8,128)(2,1)}) %reduce-scatter.9.cloned.1.call-update) | async-done | bytes 1048592 | tf_op jit(solution)/shard_map/reduce_scatter | solution.py:46
  659.1 19.0 %fusion.65 = bf16[2,1024,4,64]{1,3,2,0:T(8,128)(2,1)S(1)} fusion(bf16[2,1024,4,64]{1,0,3,2:T(2,128)(2,1)} %reshape_reshape_transpose_reshape_reshape.3, f32[2,4,1024,1024]{2,3,1,0:T(8,128)} %get-tuple-element.94, f32[2,4,1024]{2,1,0:T(4,128)S(1)} %bitcast.219, f32[4,1024,1024]{1,2,0:T(8,128)} %broadcast_multiply_fusion, ...), kind=kOutput, calls=%fused_computation.92 | convolution fusion | flops 1116209152 | bytes 54558720 | tf_op jit(solution)/shard_map/shqk,sqhe->skhe/dot_general | solution.py:86
  693.7 55.8 %fusion.68 = bf16[2,1024,4,64]{1,3,2,0:T(8,128)(2,1)} fusion(bf16[2,1024,4,64]{1,3,2,0:T(8,128)(2,1)} %copy.112, f32[2,4,1024,1024]{2,3,1,0:T(8,128)} %fusion.76, f32[2,4,1024,1024]{2,3,1,0:T(8,128)} %get-tuple-element.94, f32[2,4,1024]{2,1,0:T(4,128)S(1)} %bitcast.220, f32[4,1024,1024]{1,2,0:T(8,128)} %broadcast_multiply_fusion, ...), kind=kOutput, calls=%fused_computation.93 | convolution fusion | flops 1183327232 | bytes 88113152 | tf_op jit(solution)/shard_map/shqk,sqhe->skhe/dot_general | solution.py:85
  753.1 55.0 %fusion.71 = bf16[2,1024,4,64]{1,3,2,0:T(8,128)(2,1)} fusion(bf16[2,1024,4,64]{1,3,2,0:T(8,128)(2,1)} %copy.113, f32[2,4,1024,1024]{2,3,1,0:T(8,128)} %fusion.76, f32[2,4,1024,1024]{2,3,1,0:T(8,128)} %get-tuple-element.94, f32[2,4,1024]{2,1,0:T(4,128)S(1)} %bitcast.221, f32[4,1024,1024]{1,2,0:T(8,128)} %broadcast_multiply_fusion, ...), kind=kOutput, calls=%fused_computation.94 | convolution fusion | flops 1183327232 | bytes 88113152 | tf_op jit(solution)/shard_map/shqk,skhe->sqhe/dot_general | solution.py:84
  845.4 18.8 %all_to_all.32 = bf16[4,128,1024]{2,1,0:T(8,128)(2,1)} all-to-all(bf16[4,128,1024]{2,1,0:T(8,128)(2,1)} %bitcast.218), channel_id=1, replica_groups=mesh['rep'=2,'fsdp'=4,'ctx'=4] {'ctx'}, dimensions={0} | all-to-all | bytes 2097152 | tf_op jit(solution)/shard_map/all_to_all | solution.py:140
  864.2 21.7 %reduce-scatter.15.cloned.1.call-done = bf16[512,768]{1,0:T(8,128)(2,1)} async-done(((bf16[2048,768]{1,0:T(8,128)(2,1)}), bf16[512,768]{1,0:T(8,128)(2,1)}) %reduce-scatter.15.cloned.1.call-update) | async-done | bytes 786448 | tf_op jit(solution)/shard_map/reduce_scatter | solution.py:139
  902.0 58.7 %reduce-scatter.13.cloned.1.call-done = bf16[256,2048]{1,0:T(8,128)(2,1)} async-done(((bf16[2048,2048]{1,0:T(8,128)(2,1)}), bf16[256,2048]{1,0:T(8,128)(2,1)}) %reduce-scatter.13.cloned.1.call-update) | async-done | bytes 1048592 | tf_op jit(solution)/shard_map/reduce_scatter | solution.py:46
  963.8 71.9 %reduce-scatter.17.cloned.1.call-done = bf16[256,2048]{1,0:T(8,128)(2,1)} async-done(((bf16[2048,2048]{1,0:T(8,128)(2,1)}), bf16[256,2048]{1,0:T(8,128)(2,1)}) %reduce-scatter.17.cloned.1.call-update) | async-done | bytes 1048592 | tf_op jit(solution)/shard_map/reduce_scatter | solution.py:46
  1036.3 33.9 %all-gather.28.cloned.1.call-done = bf16[512,2048]{1,0:T(8,128)(2,1)} async-done(((bf16[256,2048]{1,0:T(8,128)(2,1)}), bf16[512,2048]{1,0:T(8,128)(2,1)}) %all-gather.28.cloned.1.call-update) | async-done | bytes 2097168 | tf_op jit(solution)/shard_map/all_gather | solution.py:153
  1074.4 30.4 %all-gather.34.cloned.1.call-done = bf16[8,128,1024]{2,1,0:T(8,128)(2,1)} async-done(((bf16[4,128,1024]{2,1,0:T(8,128)(2,1)}), bf16[8,128,1024]{2,1,0:T(8,128)(2,1)}) %all-gather.34.cloned.1.call-update) | async-done | bytes 2097168 | tf_op jit(solution)/shard_map/all_gather | solution.py:141
  1145.5 79.0 %all-reduce.4.cloned.1.call-done = f32[16,1536]{1,0:T(8,128)} async-done(((f32[16,1536]{1,0:T(8,128)}), f32[16,1536]{1,0:T(8,128)}) %all-reduce.4.cloned.1.call-update) | async-done | bytes 98320
  1232.0 21.0 %reduce-scatter.19.cloned.1.call-done = bf16[64,2048]{1,0:T(8,128)(2,1)} async-done(((bf16[256,2048]{1,0:T(8,128)(2,1)}), bf16[64,2048]{1,0:T(8,128)(2,1)}) %reduce-scatter.19.cloned.1.call-update) | async-done | bytes 262160 | tf_op jit(solution)/shard_map/reduce_scatter | solution.py:266
  (280 shorter events, 357.7 us)
Async XLA Ops:
  7.3 46.4 %all-gather.20.cloned.1.call-start = ((), (), s32[]{:S(2)}) async-start(), calls=%async_computation.16 | async-start | bytes 1310720 | tf_op jit(solution)/shard_map/all_gather | solution.py:189
  9.0 97.5 %all-gather.18.cloned.1.call-start = ((), (), s32[]{:S(2)}) async-start(), calls=%async_computation.15 | async-start | bytes 3932160 | tf_op jit(solution)/shard_map/all_gather | solution.py:136
  28.0 134.0 %all-gather.16.cloned.1.call-start = ((), (), s32[]{:S(2)}) async-start(), calls=%async_computation.14 | async-start | bytes 9437184 | tf_op jit(solution)/shard_map/all_gather | solution.py:42
  53.6 228.7 %all-gather.22.cloned.1.call-start = ((), (), s32[]{:S(2)}) async-start(), calls=%async_computation.17 | async-start | bytes 9437184 | tf_op jit(solution)/shard_map/all_gather | solution.py:42
  61.3 23.3 %all-to-all-start.2 = ((bf16[4,128,1024]{1,2,0:T(8,128)(2,1)}), bf16[4,128,1024]{1,2,0:T(8,128)(2,1)}, u32[]{:S(2)}, u32[]{:S(2)}) async-start(bf16[4,128,1024]{1,2,0:T(8,128)(2,1)} %bitcast.20), calls=%async_computation.2 | async-start | bytes 2097152 | tf_op jit(solution)/shard_map/all_to_all | solution.py:135
  65.6 360.7 %all-gather.26.cloned.1.call-start = ((), (), s32[]{:S(2)}) async-start(), calls=%async_computation.19 | async-start | bytes 5242880 | tf_op jit(solution)/shard_map/all_gather | solution.py:136
  86.9 339.4 %all-gather.24.cloned.1.call-start = ((), (), s32[]{:S(2)}) async-start(), calls=%async_computation.18 | async-start | bytes 9437184 | tf_op jit(solution)/shard_map/all_gather | solution.py:42
  291.5 150.7 %all-gather.30.cloned.1.call-start = ((), (), s32[]{:S(2)}) async-start(), calls=%async_computation.29 | async-start | bytes 9437184 | tf_op jit(solution)/shard_map/all_gather | solution.py:42
  292.2 251.3 %reduce-scatter.11.cloned.1.call-start = ((), (), s32[]{:S(2)}) async-start(), calls=%async_computation.21 | async-start | bytes 9437184 | tf_op jit(solution)/shard_map/reduce_scatter | solution.py:46
  294.7 27.2 %collective-permute-start = (bf16[256,2048]{1,0:T(8,128)(2,1)S(1)}, bf16[256,2048]{1,0:T(8,128)(2,1)S(1)}, u32[]{:S(2)}, u32[]{:S(2)}) collective-permute-start(bf16[256,2048]{1,0:T(8,128)(2,1)S(1)} %get-tuple-element.71), channel_id=1, source_target_pairs={{0,12},{4,0},{8,4},{12,8},{1,13},{5,1},{9,5},{13,9},{2,14},{6,2},{... | collective-permute-start | bytes 3145736 | tf_op jit(solution)/shard_map/ppermute | solution.py:197
  323.6 92.9 %collective-permute-start.1 = (bf16[512,2048]{1,0:T(8,128)(2,1)}, bf16[512,2048]{1,0:T(8,128)(2,1)}, u32[]{:S(2)}, u32[]{:S(2)}) collective-permute-start(bf16[512,2048]{1,0:T(8,128)(2,1)} %pad_maximum_fusion), channel_id=1, source_target_pairs={{0,8},{4,12},{8,0},{12,4},{1,9},{5,13},{9,1},{13,5},{2,10},{6,14},... | collective-permute-start | bytes 6291464 | tf_op jit(solution)/shard_map/ppermute | solution.py:197
  472.1 146.6 %reduce-scatter.9.cloned.1.call-start = ((), (), s32[]{:S(2)}) async-start(), calls=%async_computation.20 | async-start | bytes 9437184 | tf_op jit(solution)/shard_map/reduce_scatter | solution.py:46
  486.8 357.9 %reduce-scatter.23.cloned.1.call-start = ((), (), s32[]{:S(2)}) async-start(), calls=%async_computation.27 | async-start | bytes 5242880 | tf_op jit(solution)/shard_map/reduce_scatter | solution.py:262
  635.3 18.7 %all-to-all-start.3 = ((bf16[8,256,256]{1,2,0:T(8,128)(2,1)}), bf16[8,256,256]{1,2,0:T(8,128)(2,1)}, u32[]{:S(2)}, u32[]{:S(2)}) async-start(bf16[8,256,256]{1,2,0:T(8,128)(2,1)} %bitcast.208), calls=%async_computation.5 | async-start | bytes 2097152 | tf_op jit(solution)/shard_map/all_to_all | solution.py:50
  639.6 205.8 %reduce-scatter.21.cloned.1.call-start = ((), (), s32[]{:S(2)}) async-start(), calls=%async_computation.26 | async-start | bytes 5242880 | tf_op jit(solution)/shard_map/reduce_scatter | solution.py:139
  653.9 232.0 %reduce-scatter.15.cloned.1.call-start = ((), (), s32[]{:S(2)}) async-start(), calls=%async_computation.23 | async-start | bytes 3932160 | tf_op jit(solution)/shard_map/reduce_scatter | solution.py:139
  824.3 136.4 %reduce-scatter.13.cloned.1.call-start = ((), (), s32[]{:S(2)}) async-start(), calls=%async_computation.22 | async-start | bytes 9437184 | tf_op jit(solution)/shard_map/reduce_scatter | solution.py:46
  836.2 199.5 %reduce-scatter.17.cloned.1.call-start = ((), (), s32[]{:S(2)}) async-start(), calls=%async_computation.24 | async-start | bytes 9437184 | tf_op jit(solution)/shard_map/reduce_scatter | solution.py:46
  844.7 225.5 %all-gather.28.cloned.1.call-start = ((), (), s32[]{:S(2)}) async-start(), calls=%async_computation.28 | async-start | bytes 3145728 | tf_op jit(solution)/shard_map/all_gather | solution.py:153
  845.3 259.5 %all-gather.34.cloned.1.call-start = ((), (), s32[]{:S(2)}) async-start(), calls=%async_computation.31 | async-start | bytes 3145728 | tf_op jit(solution)/shard_map/all_gather | solution.py:141
  885.9 15.1 %all-to-all-start.4 = ((bf16[4,128,768]{2,1,0:T(8,128)(2,1)}), bf16[4,128,768]{2,1,0:T(8,128)(2,1)S(1)}, u32[]{:S(2)}, u32[]{:S(2)}) async-start(bf16[4,128,768]{2,1,0:T(8,128)(2,1)} %bitcast.222), calls=%async_computation.8 | async-start | bytes 1572864 | tf_op jit(solution)/shard_map/all_to_all | solution.py:140
  889.4 244.6 %all-gather.32.cloned.1.call-start = ((), (), s32[]{:S(2)}) async-start(), calls=%async_computation.30 | async-start | bytes 2359296 | tf_op jit(solution)/shard_map/all_gather | solution.py:141
  901.9 322.6 %all-reduce.4.cloned.1.call-start = ((), (), s32[]{:S(2)}) async-start(), calls=%async_computation.32 | async-start | bytes 196608
  963.8 289.3 %reduce-scatter.19.cloned.1.call-start = ((), (), s32[]{:S(2)}) async-start(), calls=%async_computation.25 | async-start | bytes 1310720 | tf_op jit(solution)/shard_map/reduce_scatter | solution.py:266
  (43 other events, 1866.7 us)
Sparse Core Ops, SparseCore 0:
  10.3 31.0 all-gather.19
  43.5 62.9 all-gather.17
  108.9 53.0 all-gather.15
  163.7 54.3 all-gather.21
  220.1 83.0 all-gather.25
  305.6 53.5 all-gather.23
  361.0 54.3 all-gather.29
  472.3 71.2 reduce-scatter.10
  547.4 71.2 reduce-scatter.8
  620.8 76.7 reduce-scatter.22
  700.6 77.2 reduce-scatter.20
  824.4 61.4 reduce-scatter.14
  889.3 71.2 reduce-scatter.12
  964.4 71.2 reduce-scatter.16
  1037.1 33.1 all-gather.27
  1071.6 33.1 all-gather.33
  1106.8 27.1 all-gather.31
  1137.3 87.1 all-reduce.3
  1226.9 26.1 reduce-scatter.18
